TPU v7x, 128 devices: a whole 4x4x4 slice. The times are simulated.
128 devices in a mesh: gx: 8 (over y, z_lo), gz: 16 (over z_hi, x, core).
Axes of the slice: x: 4, y: 4, z: 4 (z_hi: 2, z_lo: 2; z = z_hi * 2 + z_lo), core: 2. Of those that a mesh axis runs over, the one named last changes fastest.
Arguments:
- velocity: float32 [3, 2048, 8, 4096], P(None, 'gx', None, 'gz'), may hold values from -6 to 6
- prior: float32 [3, 2048, 8, 4096], P(None, 'gx', None, 'gz'), may hold values from -3 to 3
Outputs:
- filtered: float32 [3, 2048, 8, 4096], P(None, 'gx', None, 'gz')
- advance: float32 [3, 2048, 8, 4096], P(None, 'gx', None, 'gz')
All inputs are finite; a program needn't handle non-finite values.
Results may differ from a plain program's by a relative error of at most 0.0003.
Values sent between devices are 32-bit elements; how exact they have to be, the bound alone decides.
No kernel may reach another device: no remote copies, remote signals or barrier semaphores. Data moves between devices by JAX's collectives and lax.ppermute only.
A program may use at most 128 MiB of HBM per device.

v0:
```python
import math

import jax
import jax.numpy as jnp
import numpy as np
from jax import lax
from jax.sharding import PartitionSpec as P

alpha_deriv = 1.0 / 3.0
alpha_filter = 0.49
reach_deriv = 24
reach_filter = 72
highest = lax.Precision.HIGHEST


def extended(block, sides, width):
    for axis, dim in sides:
        count = lax.axis_size(axis)
        forward = [(i, i + 1) for i in range(count - 1)]
        forward.append((count - 1, 0))
        backward = [(target, source) for source, target in forward]
        low = lax.ppermute(
            lax.slice_in_dim(block, block.shape[dim] - width, None, axis=dim), axis, forward
        )
        high = lax.ppermute(lax.slice_in_dim(block, 0, width, axis=dim), axis, backward)
        block = jnp.concatenate([low, block, high], axis=dim)
    return block


def decay_rate(alpha):
    return (-1.0 + math.sqrt(1.0 - 4.0 * alpha * alpha)) / (2.0 * alpha)


def green_scale(alpha):
    return 1.0 / (1.0 + 2.0 * alpha * decay_rate(alpha))


def green_lookup(count, extent, offset, alpha):
    targets = np.arange(count)[:, None]
    sources = np.arange(extent)[None, :] - offset
    values = green_scale(alpha) * np.power(decay_rate(alpha), np.abs(targets - sources))
    return jnp.asarray(values, dtype=jnp.float32)


def along(lookup, values, axis):
    if axis == 1:
        return jnp.einsum("st,ctyz->csyz", lookup, values, precision=highest)
    return jnp.einsum("cxyt,st->cxys", values, lookup, precision=highest)


def shifted(values, start, count, axis):
    return lax.slice_in_dim(values, start, start + count, axis=axis)


def deriv_terms(padded, count, axis, spacing):
    ahead = shifted(padded, 3, count, axis) - shifted(padded, 1, count, axis)
    further = shifted(padded, 4, count, axis) - shifted(padded, 0, count, axis)
    return 14.0 / 9.0 * ahead / (2.0 * spacing) + 1.0 / 9.0 * further / (4.0 * spacing)


def filter_terms(padded, count, axis):
    weights = [
        (11.0 + 10.0 * alpha_filter) / 16.0,
        (15.0 + 34.0 * alpha_filter) / 32.0,
        (-3.0 + 6.0 * alpha_filter) / 16.0,
        (1.0 - 2.0 * alpha_filter) / 32.0,
    ]
    total = weights[0] * shifted(padded, 3, count, axis)
    for offset in range(1, 4):
        total = total + 0.5 * weights[offset] * (
            shifted(padded, 3 + offset, count, axis) + shifted(padded, 3 - offset, count, axis)
        )
    return total


def axial_edge(values, width):
    return extended(values, (("gx", 1),), width)


def lateral_edge(values, width):
    return extended(values, (("gz", 3),), width)


def edge_along(values, width, axis):
    if axis == 1:
        return axial_edge(values, width)
    return lateral_edge(values, width)


def margin_solve(padded, count, reach, alpha, axis, kind, spacing):
    extent = count + 2 * reach
    if kind == 0:
        terms = deriv_terms(padded, extent, axis, spacing)
    else:
        terms = filter_terms(padded, extent, axis)
    return along(green_lookup(count, extent, reach, alpha), terms, axis)


def shards(velocity, prior):
    cells_x = velocity.shape[1]
    cells_z = velocity.shape[3]
    spacing_x = 8.0 * math.pi / (cells_x * lax.axis_size("gx"))
    spacing_z = 3.0 * math.pi / (cells_z * lax.axis_size("gz"))
    dt_step = 0.3 / (1.0 / spacing_x + 1.0 / spacing_z)
    grad_x = margin_solve(
        edge_along(velocity, 2 + reach_deriv, 1), cells_x, reach_deriv, alpha_deriv, 1, 0, spacing_x
    )
    grad_z = margin_solve(
        edge_along(velocity, 2 + reach_deriv, 3), cells_z, reach_deriv, alpha_deriv, 3, 0, spacing_z
    )
    advance = -dt_step * (velocity[0:1] * grad_x + velocity[2:3] * grad_z)
    provisional = velocity + 5.0 / 12.0 * advance - 17.0 / 60.0 * prior
    across = margin_solve(
        edge_along(provisional, 3 + reach_filter, 1),
        cells_x,
        reach_filter,
        alpha_filter,
        1,
        1,
        spacing_x,
    )
    filtered = margin_solve(
        edge_along(across, 3 + reach_filter, 3),
        cells_z,
        reach_filter,
        alpha_filter,
        3,
        1,
        spacing_z,
    )
    return (filtered, advance)


def solution(mesh):
    placed = (P(None, "gx", None, "gz"), P(None, "gx", None, "gz"))
    return jax.shard_map(
        shards,
        mesh=mesh,
        in_specs=placed,
        out_specs=(P(None, "gx", None, "gz"), P(None, "gx", None, "gz")),
        check_vma=False,
    )
```

profile of v0, /device:TPU:0, one launch (start us, length us, event | category | flops | bytes accessed | tf_op | source)
XLA Modules:
  0.0 387.6 jit_solution(10406841654986242585)
XLA Ops:
  0.6 5.4 %fusion.47 = (f32[3,256,8,26]{3,2,1,0:T(8,128)}, f32[3,256,8,26]{3,2,1,0:T(8,128)S(1)}) fusion(f32[3,256,8,256]{3,2,1,0:T(8,128)} %param.6), kind=kLoop, calls=%fused_computation.64 | loop fusion | bytes 2555904 | tf_op jit(solution)/shard_map/slice | solution.py:23
  6.0 3.1 copy.40
  9.2 2.4 fusion.46
  11.6 2.0 collective-permute-start
  13.6 2.5 collective-permute-start.1
  18.0 5.8 %collective-permute-start.3 = (f32[3,256,8,26]{1,2,3,0:T(8,128)}, f32[3,256,8,26]{1,2,3,0:T(8,128)}, u32[]{:S(2)}, u32[]{:S(2)}) collective-permute-start(f32[3,256,8,26]{1,2,3,0:T(8,128)} %copy.41), channel_id=1, source_target_pairs={{1,0},{2,1},{3,2},{4,3},{5,4},{6,5},{7,6},{8,7},{9,8},{10,9},{11,1... | collective-permute-start | bytes 1916936 | tf_op jit(solution)/shard_map/ppermute | solution.py:25
  23.8 2.5 slice_bitcast_fusion.1
  28.3 2.0 copy.18
  30.3 2.1 copy.21
  32.4 16.2 %collective-permute-done = f32[3,26,8,256]{3,2,1,0:T(8,128)} collective-permute-done((f32[3,26,8,256]{3,2,1,0:T(8,128)}, f32[3,26,8,256]{3,2,1,0:T(8,128)}, u32[]{:S(2)}, u32[]{:S(2)}) %collective-permute-start) | collective-permute-done | bytes 639008 | tf_op jit(solution)/shard_map/ppermute | solution.py:22
  48.6 2.0 constant_dynamic-update-slice_fusion.2
  50.6 5.8 %constant_dynamic-update-slice_fusion.1 = f32[3,308,8,256]{3,2,1,0:T(8,128)} fusion(f32[3,308,8,256]{3,2,1,0:T(8,128)} %constant_dynamic-update-slice_fusion.2, f32[3,256,8,256]{3,2,1,0:T(8,128)} %param.6), kind=kLoop, calls=%fused_computation.55 | loop fusion | bytes 12582912
  56.4 3.1 copy.22
  59.5 10.7 %pad_maximum_fusion.2 = f32[3,256,8,308]{3,2,1,0:T(8,128)} fusion(f32[3,256,8,26]{3,2,1,0:T(8,128)} %copy.22, f32[3,256,8,256]{3,2,1,0:T(8,128)} %param.6, f32[3,256,8,26]{3,2,1,0:T(8,128)S(1)} %copy.21), kind=kLoop, calls=%fused_computation.31 | loop fusion | flops 3784704 | bytes 15138816 | tf_op jit(solution)/shard_map/concatenate | solution.py:26
  70.2 18.2 %fusion.20 = f32[3,256,8,304]{3,2,1,0:T(8,128)S(1)} fusion(f32[3,256,8,308]{3,2,1,0:T(8,128)} %pad_maximum_fusion.2), kind=kLoop, calls=%fused_computation.28 | loop fusion | flops 9338880 | bytes 37355520 | tf_op jit(solution)/shard_map/add | solution.py:58
  90.5 13.9 %fusion.25 = f32[3,304,8,256]{3,2,1,0:T(8,128)} fusion(f32[3,308,8,256]{3,2,1,0:T(8,128)} %constant_dynamic-update-slice_fusion), kind=kLoop, calls=%fused_computation.36 | loop fusion | flops 9338880 | bytes 37355520 | tf_op jit(solution)/shard_map/add | solution.py:58
  104.4 12.8 %fusion.22 = f32[3,256,8,256]{3,1,2,0:T(8,128)} fusion(f32[256,304,1,1]{0,1,3,2:T(8,128)S(1)} %copy-done, f32[3,256,8,304]{3,2,1,0:T(8,128)S(1)} %fusion.20), kind=kOutput, calls=%fused_computation.32 | convolution fusion | flops 5737807872 | bytes 14073856 | tf_op jit(solution)/shard_map/cxyt,st->cxys/dot_general | solution.py:48
  117.2 29.5 %broadcast_multiply_fusion = (f32[3,256,8,256]{3,1,2,0:T(8,128)}, f32[3,256,8,256]{3,1,2,0:T(8,128)}) fusion(f32[3,256,8,256]{3,2,1,0:T(8,128)} %param.7, f32[3,256,8,256]{3,2,1,0:T(8,128)S(1)} %bitcast.22, f32[3,256,8,256]{3,1,2,0:T(8,128)} %fusion.22, f32[256,8,256]{2,0,1:T(8,128)} %copy.18, f32[256,304,1,1]{0,1,3,2:T(8,128)S(1)} %copy-done, ...), kind=kOutput, calls=%fused_computation.50 | convolution fusion | flops 5750390784 | bytes 43433984 | tf_op jit(solution)/shard_map/st,ctyz->csyz/dot_general | solution.py:47
  146.8 2.6 fusion.45
  150.4 5.0 %collective-permute-start.5 = (f32[3,75,8,256]{3,2,1,0:T(8,128)S(1)}, f32[3,75,8,256]{3,2,1,0:T(8,128)S(1)}, u32[]{:S(2)}, u32[]{:S(2)}) collective-permute-start(f32[3,75,8,256]{3,2,1,0:T(8,128)S(1)} %copy.27), channel_id=1, source_target_pairs={{16,0},{32,16},{48,32},{64,48},{80,64},{96,80},{112,96},{0,112},{1... | collective-permute-start | bytes 5529608 | tf_op jit(solution)/shard_map/ppermute | solution.py:25
  156.6 76.7 %collective-permute-done.5 = f32[3,75,8,256]{3,2,1,0:T(8,128)S(1)} collective-permute-done((f32[3,75,8,256]{3,2,1,0:T(8,128)S(1)}, f32[3,75,8,256]{3,2,1,0:T(8,128)S(1)}, u32[]{:S(2)}, u32[]{:S(2)}) %collective-permute-start.5) | collective-permute-done | bytes 1843232 | tf_op jit(solution)/shard_map/ppermute | solution.py:25
  235.7 8.2 %pad_maximum_fusion = f32[3,406,8,256]{3,1,2,0:T(8,128)} fusion(f32[3,75,8,256]{3,1,2,0:T(8,128)S(1)} %copy.29, f32[3,256,8,256]{3,1,2,0:T(8,128)} %get-tuple-element.7, f32[3,75,8,256]{3,1,2,0:T(8,128)} %copy.28), kind=kLoop, calls=%fused_computation | loop fusion | flops 4988928 | bytes 19955712 | tf_op jit(solution)/shard_map/concatenate | solution.py:26
  243.9 40.3 %fusion.37 = f32[3,256,8,256]{1,3,2,0:T(8,128)} fusion(f32[256,400,1,1]{0,1,3,2:T(8,128)S(1)} %copy-done.1, f32[3,406,8,256]{3,1,2,0:T(8,128)} %pad_maximum_fusion), kind=kOutput, calls=%fused_computation.51 | convolution fusion | flops 7574323200 | bytes 75513856 | tf_op jit(solution)/shard_map/st,ctyz->csyz/dot_general | solution.py:47
  284.2 2.6 fusion.44
  287.9 4.5 %collective-permute-start.7 = (f32[3,256,8,75]{1,2,3,0:T(8,128)S(1)}, f32[3,256,8,75]{1,2,3,0:T(8,128)S(1)}, u32[]{:S(2)}, u32[]{:S(2)}) collective-permute-start(f32[3,256,8,75]{1,2,3,0:T(8,128)S(1)} %copy.31), channel_id=1, source_target_pairs={{1,0},{2,1},{3,2},{4,3},{5,4},{6,5},{7,6},{8,7},{9,8},{10,9},{11,1... | collective-permute-start | bytes 5529608 | tf_op jit(solution)/shard_map/ppermute | solution.py:25
  293.7 9.1 %copy.35 = f32[3,256,8,256]{3,2,1,0:T(8,128)} copy(f32[3,256,8,256]{3,1,2,0:T(8,128)} %get-tuple-element.6) | data formatting | bytes 12582912
  302.9 10.3 %collective-permute-done.7 = f32[3,256,8,75]{1,2,3,0:T(8,128)S(1)} collective-permute-done((f32[3,256,8,75]{1,2,3,0:T(8,128)S(1)}, f32[3,256,8,75]{1,2,3,0:T(8,128)S(1)}, u32[]{:S(2)}, u32[]{:S(2)}) %collective-permute-start.7) | collective-permute-done | bytes 1843232 | tf_op jit(solution)/shard_map/ppermute | solution.py:25
  313.8 6.3 %collective-permute-done.6 = f32[3,256,8,75]{1,2,3,0:T(8,128)S(1)} collective-permute-done((f32[3,256,8,75]{1,2,3,0:T(8,128)S(1)}, f32[3,256,8,75]{1,2,3,0:T(8,128)S(1)}, u32[]{:S(2)}, u32[]{:S(2)}) %collective-permute-start.6) | collective-permute-done | bytes 1843232 | tf_op jit(solution)/shard_map/ppermute | solution.py:22
  321.9 8.2 %pad_maximum_fusion.1 = f32[3,256,8,406]{1,3,2,0:T(8,128)} fusion(f32[3,256,8,75]{1,3,2,0:T(8,128)S(1)} %copy.33, f32[3,256,8,256]{1,3,2,0:T(8,128)} %fusion.37, f32[3,256,8,75]{1,3,2,0:T(8,128)} %copy.32), kind=kLoop, calls=%fused_computation.1 | loop fusion | flops 4988928 | bytes 19955712 | tf_op jit(solution)/shard_map/concatenate | solution.py:26
  330.1 30.1 %fusion.1 = f32[3,256,8,400]{1,3,2,0:T(8,128)} fusion(f32[3,256,8,406]{1,3,2,0:T(8,128)} %pad_maximum_fusion.1), kind=kLoop, calls=%fused_computation.4 | loop fusion | flops 24576000 | bytes 78643200 | tf_op jit(solution)/shard_map/add | solution.py:70
  360.2 12.8 %copy.38 = f32[3,256,8,400]{3,2,1,0:T(8,128)} copy(f32[3,256,8,400]{1,3,2,0:T(8,128)} %fusion.1) | data formatting | bytes 19660800 | tf_op jit(solution)/shard_map/add | solution.py:70
  373.0 14.3 %fusion.48 = f32[3,256,8,256]{3,2,1,0:T(8,128)} fusion(f32[3,256,8,400]{3,2,1,0:T(8,128)} %copy.38, f32[256,400,1,1]{0,1,3,2:T(8,128)S(1)} %copy-done.1), kind=kOutput, calls=%fused_computation.65 | convolution fusion | flops 7549747200 | bytes 16531456 | tf_op jit(solution)/shard_map/cxyt,st->cxys/dot_general | solution.py:48
  (27 shorter events, 15.4 us)
Async XLA Ops:
  9.1 21.1 %collective-permute-start.2 = (f32[3,256,8,26]{1,2,3,0:T(8,128)}, f32[3,256,8,26]{1,2,3,0:T(8,128)}, u32[]{:S(2)}, u32[]{:S(2)}) collective-permute-start(f32[3,256,8,26]{1,2,3,0:T(8,128)} %copy.40), channel_id=1, source_target_pairs={{0,1},{1,2},{2,3},{3,4},{4,5},{5,6},{6,7},{7,8},{8,9},{9,10},{10,1... | collective-permute-start | bytes 1916936 | tf_op jit(solution)/shard_map/ppermute | solution.py:22
  11.6 37.0 %collective-permute-start = (f32[3,26,8,256]{3,2,1,0:T(8,128)}, f32[3,26,8,256]{3,2,1,0:T(8,128)}, u32[]{:S(2)}, u32[]{:S(2)}) collective-permute-start(f32[3,26,8,256]{3,2,1,0:T(8,128)} %get-tuple-element.13), channel_id=1, source_target_pairs={{0,16},{16,32},{32,48},{48,64},{64,80},{80,96},{96,112},{112,0},{1... | collective-permute-start | bytes 1916936 | tf_op jit(solution)/shard_map/ppermute | solution.py:22
  13.6 74.9 %collective-permute-start.1 = (f32[3,26,8,256]{3,2,1,0:T(8,128)}, f32[3,26,8,256]{3,2,1,0:T(8,128)}, u32[]{:S(2)}, u32[]{:S(2)}) collective-permute-start(f32[3,26,8,256]{3,2,1,0:T(8,128)} %get-tuple-element.12), channel_id=1, source_target_pairs={{16,0},{32,16},{48,32},{64,48},{80,64},{96,80},{112,96},{0,112},{1... | collective-permute-start | bytes 1916936 | tf_op jit(solution)/shard_map/ppermute | solution.py:25
  18.0 38.4 %collective-permute-start.3 = (f32[3,256,8,26]{1,2,3,0:T(8,128)}, f32[3,256,8,26]{1,2,3,0:T(8,128)}, u32[]{:S(2)}, u32[]{:S(2)}) collective-permute-start(f32[3,256,8,26]{1,2,3,0:T(8,128)} %copy.41), channel_id=1, source_target_pairs={{1,0},{2,1},{3,2},{4,3},{5,4},{6,5},{7,6},{8,7},{9,8},{10,9},{11,1... | collective-permute-start | bytes 1916936 | tf_op jit(solution)/shard_map/ppermute | solution.py:25
  70.2 47.0 %slice-start = ((s8[6291456]{0:T(1024)(128)(4,1)}), s8[4194304]{0:T(1024)(128)(4,1)S(1)}, s32[]{:S(2)}) async-start(s8[6291456]{0:T(1024)(128)(4,1)} %bitcast.21), calls=%async_computation | async-start | bytes 8388608
  90.5 13.9 %copy-start = (f32[256,304,1,1]{0,1,3,2:T(8,128)S(1)}, f32[256,304,1,1]{0,1,3,2:T(8,128)}, u32[]{:S(2)}) copy-start(f32[256,304,1,1]{0,1,3,2:T(8,128)} %constant.45) | copy-start | bytes 933892
  90.5 26.7 %slice-start.1 = ((s8[6291456]{0:T(1024)(128)(4,1)}), s8[2097152]{0:T(1024)(128)(4,1)S(1)}, s32[]{:S(2)}) async-start(s8[6291456]{0:T(1024)(128)(4,1)} %bitcast.21), calls=%async_computation.1 | async-start | bytes 4194304
  150.4 82.9 %collective-permute-start.5 = (f32[3,75,8,256]{3,2,1,0:T(8,128)S(1)}, f32[3,75,8,256]{3,2,1,0:T(8,128)S(1)}, u32[]{:S(2)}, u32[]{:S(2)}) collective-permute-start(f32[3,75,8,256]{3,2,1,0:T(8,128)S(1)} %copy.27), channel_id=1, source_target_pairs={{16,0},{32,16},{48,32},{64,48},{80,64},{96,80},{112,96},{0,112},{1... | collective-permute-start | bytes 5529608 | tf_op jit(solution)/shard_map/ppermute | solution.py:25
  156.5 77.4 %collective-permute-start.4 = (f32[3,75,8,256]{3,2,1,0:T(8,128)S(1)}, f32[3,75,8,256]{3,2,1,0:T(8,128)S(1)}, u32[]{:S(2)}, u32[]{:S(2)}) collective-permute-start(f32[3,75,8,256]{3,2,1,0:T(8,128)S(1)} %copy.26), channel_id=1, source_target_pairs={{0,16},{16,32},{32,48},{48,64},{64,80},{80,96},{96,112},{112,0},{1... | collective-permute-start | bytes 5529608 | tf_op jit(solution)/shard_map/ppermute | solution.py:22
  235.7 8.2 %copy-start.1 = (f32[256,400,1,1]{0,1,3,2:T(8,128)S(1)}, f32[256,400,1,1]{0,1,3,2:T(8,128)}, u32[]{:S(2)}) copy-start(f32[256,400,1,1]{0,1,3,2:T(8,128)} %constant.46) | copy-start | bytes 1228804
  287.9 25.4 %collective-permute-start.7 = (f32[3,256,8,75]{1,2,3,0:T(8,128)S(1)}, f32[3,256,8,75]{1,2,3,0:T(8,128)S(1)}, u32[]{:S(2)}, u32[]{:S(2)}) collective-permute-start(f32[3,256,8,75]{1,2,3,0:T(8,128)S(1)} %copy.31), channel_id=1, source_target_pairs={{1,0},{2,1},{3,2},{4,3},{5,4},{6,5},{7,6},{8,7},{9,8},{10,9},{11,1... | collective-permute-start | bytes 5529608 | tf_op jit(solution)/shard_map/ppermute | solution.py:25
  293.5 26.6 %collective-permute-start.6 = (f32[3,256,8,75]{1,2,3,0:T(8,128)S(1)}, f32[3,256,8,75]{1,2,3,0:T(8,128)S(1)}, u32[]{:S(2)}, u32[]{:S(2)}) collective-permute-start(f32[3,256,8,75]{1,2,3,0:T(8,128)S(1)} %copy.30), channel_id=1, source_target_pairs={{0,1},{1,2},{2,3},{3,4},{4,5},{5,6},{6,7},{7,8},{8,9},{9,10},{10,1... | collective-permute-start | bytes 5529608 | tf_op jit(solution)/shard_map/ppermute | solution.py:22
where the time goes:
time: 391 us; the launch traced here: 388 us
  waiting for transfers between devices  110 us (28%)
  matrix products  96.9 us (25%)
  other arithmetic  89.3 us (23%)
  local copies, waits for them, and re-layouts  70.6 us (18%)
  starting transfers between devices  20.2 us (5%)
    ppermute x4, waiting for transfers between devices, extended(): lax.ppermute(lax.slice_in_dim(block, 0, width, axis=dim), axis, backward)  87 us
    dot_general x2, matrix products, along(): return jnp.einsum('st,ctyz->csyz', lookup, values, precision=highest)  69.8 us
    add x2, other arithmetic, deriv_terms(): 14.0 / 9.0 * ahead / (2.0 * spacing) + 1.0 / 9.0 * further / (4.0 * spacing)  32.1 us
    add x1, other arithmetic, filter_terms(): total + 0.5 * weights[offset] * (shifted(padded, 3 + offset, count, axis)...  30.1 us
    dot_general x2, matrix products, along(): return jnp.einsum('cxyt,st->cxys', values, lookup, precision=highest)  27.1 us
    concatenate x3, other arithmetic, extended(): block = jnp.concatenate([low, block, high], axis=dim)  27.1 us
    ppermute x4, waiting for transfers between devices, extended(): lax.ppermute(lax.slice_in_dim(block, block.shape[dim] - width, None, axis...  22.5 us
    unnamed x13, local copies, waits for them, and re-layouts  22 us
  transfers between devices with their start and end apart: 8, of which 4 were waited for; matrix products, arithmetic and copies ran while one was open for 17% of the time, Pallas kernels for 0%

commit v1 on v0

v1 whole, which is shorter than its diff:
```python
import functools
import math

import jax
import jax.numpy as jnp
import numpy as np
from jax import lax
from jax.experimental import pallas as pl
from jax.experimental.pallas import tpu as pltpu
from jax.sharding import PartitionSpec as P

alpha_deriv = 1.0 / 3.0
alpha_filter = 0.49
rows_block = 32
near_deriv = 32
near_filter = 96
bf16 = jnp.bfloat16
f32 = jnp.float32
highest = lax.Precision.HIGHEST


def decay_rate(alpha):
    return (-1.0 + math.sqrt(1.0 - 4.0 * alpha * alpha)) / (2.0 * alpha)


def green_scale(alpha):
    return 1.0 / (1.0 + 2.0 * alpha * decay_rate(alpha))


def kernel_values(offsets, taps, alpha):
    offsets = np.asarray(offsets, dtype=np.float64)
    total = np.zeros_like(offsets)
    for shift, weight in taps.items():
        total = total + weight * green_scale(alpha) * np.power(
            decay_rate(alpha), np.abs(offsets - shift)
        )
    return total


def deriv_taps(spacing):
    near = 14.0 / 9.0 / (2.0 * spacing)
    far = 1.0 / 9.0 / (4.0 * spacing)
    return {1: near, -1: -near, 2: far, -2: -far}


def filter_taps():
    taps = {0: (11.0 + 10.0 * alpha_filter) / 16.0}
    weights = (
        (15.0 + 34.0 * alpha_filter) / 32.0,
        (-3.0 + 6.0 * alpha_filter) / 16.0,
        (1.0 - 2.0 * alpha_filter) / 32.0,
    )
    for shift, weight in enumerate(weights, 1):
        taps[shift] = 0.5 * weight
        taps[-shift] = 0.5 * weight
    return taps


def parts(values):
    high = values.astype(bf16)
    low = (values - high.astype(f32)).astype(bf16)
    return high, low


def np_parts(values):
    values = np.asarray(values, dtype=np.float32)
    high = values.astype(bf16)
    low = (values - high.astype(np.float32)).astype(bf16)
    return high, low


def band_matrix(count, taps, alpha, factor):
    source = np.arange(count)[:, None]
    target = np.arange(count)[None, :]
    high, low = np_parts(factor * kernel_values(source - target, taps, alpha))
    return np.concatenate([high, high, low], axis=0)


def edge_functionals(count, taps, alpha, factor, terms, group):
    source = np.arange(count)
    table = np.zeros((2 * group, 3 * count))
    for term in range(terms):
        right = factor * kernel_values(source - (count + term), taps, alpha)
        left = factor * kernel_values(source + 1 + term, taps, alpha)
        for comp in range(3):
            span = slice(comp * count, (comp + 1) * count)
            table[term * 3 + comp, span] = right
            table[group + term * 3 + comp, span] = left
    return table


def edge_profiles(count, alpha, terms, group):
    cell = np.arange(count)
    table = np.zeros((3, 2 * group, count))
    rate = decay_rate(alpha)
    for term in range(terms):
        if term < terms - 1:
            shape = (cell == term) * 1.0
        else:
            shape = np.where(cell >= term, np.power(rate, np.maximum(cell - term, 0)), 0.0)
        for comp in range(3):
            table[comp, term * 3 + comp] = shape
            table[comp, group + term * 3 + comp] = shape[::-1]
    return table


def padded_profiles(table):
    high, low = np_parts(table)
    stacked = np.concatenate([high, high, low], axis=1)
    rest = np.zeros((3, 128 - stacked.shape[1], stacked.shape[2]), dtype=bf16)
    return np.concatenate([stacked, rest], axis=1)


def spread_columns(left, right):
    both = jnp.concatenate([left, right], axis=0)
    high = both.astype(bf16).astype(f32)
    low = both - high
    rest = jnp.zeros((128 - 3 * both.shape[0], both.shape[1]), f32)
    return jnp.concatenate([high, low, high, rest], axis=0).T.astype(bf16)


def contract_last(a, b):
    return lax.dot_general(a, b, (((1,), (1,)), ((), ())), preferred_element_type=f32)


def dot(a, b):
    return jnp.dot(a, b, preferred_element_type=f32)


def edge_values(functional, highs, lows, count):
    half = functional.shape[0] // 2
    first = None
    second = None
    for comp in range(3):
        span = slice(comp * count, (comp + 1) * count)
        a = contract_last(functional[:, span], highs[comp])
        b = contract_last(functional[:half, span], lows[comp])
        first = a if first is None else first + a
        second = b if second is None else second + b
    return first[:half] + first[half:] + second


def x_edge_body(rate, low_ref, high_ref, right_ref, left_ref):
    last = near_deriv - 1
    total = high_ref[:, 0]
    for i in range(1, last):
        total = rate * total + high_ref[:, i]
    right_ref[0] = total
    right_ref[1] = high_ref[:, last]
    total = low_ref[:, last]
    for i in range(last - 1, 0, -1):
        total = rate * total + low_ref[:, i]
    left_ref[0] = total
    left_ref[1] = low_ref[:, 0]


def z_edge_body(v_ref, functional_ref, right_ref, left_ref):
    rows = v_ref.shape[1] * v_ref.shape[2]
    count = v_ref.shape[3]
    highs, lows = [], []
    for comp in range(3):
        high, low = parts(v_ref[comp].reshape(rows, count))
        highs.append(high)
        lows.append(low)
    out = edge_values(functional_ref[...], highs, lows, count)
    group = right_ref.shape[0]
    right_ref[...] = out[:group]
    left_ref[...] = out[group:]


def advance_body(
    n_blocks, consts,
    v_ref, prior_ref, xl_ref, xr_ref, zl_ref, zr_ref, dz_ref, pz_ref, fz_ref, wz_ref,
    adv_ref, q_ref, zright_ref, zleft_ref, xright_ref, xleft_ref,
    back, tail, lead, prov, qlead, qback, power,
):
    step = pl.program_id(0)
    size = v_ref.shape[1]
    count = v_ref.shape[3]
    rows = size * v_ref.shape[2]
    rate = consts["rate_d"]
    ratio = consts["ratio_d"]

    @pl.when(step == 0)
    def _():
        tail[0] = xr_ref[0]
        tail[1] = xr_ref[1]

    @pl.when(step < n_blocks)
    def _():
        base = (n_blocks - 1 - step) * size
        total = tail[0]
        nxt = tail[1]
        for i in range(size - 1, -1, -1):
            back[base + i] = total + ratio * nxt
            total = rate * total + nxt
            nxt = v_ref[:, i]
        tail[0] = total
        tail[1] = nxt

    @pl.when(step == n_blocks)
    def _():
        lead[0] = xl_ref[0]
        lead[1] = xl_ref[1]
        qlead[...] = jnp.zeros_like(qlead)
        qback[...] = jnp.zeros_like(qback)
        power[0] = 1.0

    @pl.when(step >= n_blocks)
    def _():
        base = (step - n_blocks) * size
        columns = spread_columns(zl_ref[...], zr_ref[...])
        slopes = []
        for comp in range(3):
            high, low = parts(v_ref[comp].reshape(rows, count))
            lhs = jnp.concatenate([high, low, high], axis=1)
            slope = dot(lhs, dz_ref[...]) + dot(columns, pz_ref[comp])
            slopes.append(slope.reshape(size, rows // size, count))
        total = lead[0]
        prev = lead[1]
        for i in range(size):
            here = v_ref[:, i]
            gx = back[base + i] - (total + ratio * prev)
            total = rate * total + prev
            prev = here
            ux = consts["x_factor"] * here[0]
            dz = jnp.stack([slopes[comp][i] for comp in range(3)])
            adv = ux[None] * gx + here[2][None] * dz
            adv_ref[:, i] = adv
            prov[:, i] = here + (5.0 / 12.0) * adv - (17.0 / 60.0) * prior_ref[:, i]
        lead[0] = total
        lead[1] = prev
        highs, lows = [], []
        for comp in range(3):
            high, low = parts(prov[comp].reshape(rows, count))
            highs.append(high)
            lows.append(low)
            lhs = jnp.concatenate([high, low, high], axis=1)
            q_ref[comp] = dot(lhs, fz_ref[...]).reshape(size, rows // size, count)
        out = edge_values(wz_ref[...], highs, lows, count)
        group = zright_ref.shape[0]
        zright_ref[...] = out[:group]
        zleft_ref[...] = out[group:]
        rate_f = consts["rate_f"]
        total = qlead[0]
        one = qlead[1]
        two = qlead[2]
        for i in range(size):
            total = rate_f * total + two
            two = one
            one = q_ref[:, i]
        qlead[0] = total
        qlead[1] = one
        qlead[2] = two
        total = q_ref[:, size - 1]
        for i in range(size - 2, 1, -1):
            total = rate_f * total + q_ref[:, i]

        @pl.when(step == n_blocks)
        def _():
            qback[...] = total
            xleft_ref[1] = q_ref[:, 0]
            xleft_ref[2] = q_ref[:, 1]
            power[0] = consts["power_f"] / (rate_f * rate_f)

        @pl.when(step > n_blocks)
        def _():
            full = rate_f * (rate_f * total + q_ref[:, 1]) + q_ref[:, 0]
            qback[...] = qback[...] + power[0] * full
            power[0] = power[0] * consts["power_f"]

        @pl.when(step == 2 * n_blocks - 1)
        def _():
            xleft_ref[0] = qback[...]
            xright_ref[0] = qlead[0]
            xright_ref[1] = qlead[1]
            xright_ref[2] = qlead[2]


def corner_body(xright_ref, xleft_ref, zl_ref, zr_ref, tr_ref, tl_ref, pc_ref, right_ref, left_ref):
    near = tr_ref.shape[0]
    planes = jnp.concatenate([zl_ref[...], zr_ref[...]], axis=0)
    span = planes.shape[1]
    hi = jnp.dot(planes[:, span - near:], tr_ref[...], precision=highest, preferred_element_type=f32)
    lo = jnp.dot(planes[:, :near], tl_ref[...], precision=highest, preferred_element_type=f32)
    terms = right_ref.shape[0]
    lines = right_ref.shape[2]
    for comp in range(3):
        for res, src_ref, dst_ref in ((hi, xright_ref, right_ref), (lo, xleft_ref, left_ref)):
            add = lax.dot_general(
                res, pc_ref[comp], (((0,), (0,)), ((), ())),
                precision=highest, preferred_element_type=f32,
            )
            for term in range(terms):
                dst_ref[term, comp] = src_ref[term, comp] + add[term * lines:(term + 1) * lines]


def filter_body(
    n_blocks, consts,
    q_ref, xl_ref, xr_ref, zl_ref, zr_ref, pz_ref,
    out_ref,
    full, back, tail, lead,
):
    step = pl.program_id(0)
    size = q_ref.shape[1]
    count = q_ref.shape[3]
    lines = q_ref.shape[2]
    rate = consts["rate_f"]

    @pl.when(step == 0)
    def _():
        for k in range(3):
            tail[k] = xr_ref[k]
        full[n_blocks * size] = xr_ref[1]
        full[n_blocks * size + 1] = xr_ref[2]

    @pl.when(step < n_blocks)
    def _():
        base = (n_blocks - 1 - step) * size
        columns = spread_columns(zl_ref[...], zr_ref[...])
        adds = [dot(columns, pz_ref[comp]).reshape(size, lines, count) for comp in range(3)]
        total, one, two = tail[0], tail[1], tail[2]
        for i in range(size - 1, -1, -1):
            back[base + i] = total
            here = q_ref[:, i] + jnp.stack([adds[comp][i] for comp in range(3)])
            full[base + i] = here
            total = rate * total + two
            two = one
            one = here
        tail[0] = total
        tail[1] = one
        tail[2] = two

    @pl.when(step == n_blocks)
    def _():
        for k in range(3):
            lead[k] = xl_ref[k]

    @pl.when(step >= n_blocks)
    def _():
        base = (step - n_blocks) * size
        total, one, two = lead[0], lead[1], lead[2]
        here = full[base]
        ahead = full[base + 1]
        for i in range(size):
            further = full[base + i + 2]
            value = (
                consts["k3"] * (total + back[base + i])
                + consts["k0"] * here
                + consts["k1"] * (ahead + one)
                + consts["k2"] * (further + two)
            )
            out_ref[:, i] = value
            total = rate * total + two
            two = one
            one = here
            here = ahead
            ahead = further
        lead[0] = total
        lead[1] = one
        lead[2] = two


def whole(shape):
    return pl.BlockSpec(shape, lambda t: (0,) * len(shape))


def ring(count, step):
    return [(i, (i + step) % count) for i in range(count)]


def swap(right, left, axis):
    count = lax.axis_size(axis)
    return (
        lax.ppermute(right, axis, ring(count, 1)),
        lax.ppermute(left, axis, ring(count, -1)),
    )


def shards(velocity, prior):
    comps, cells_x, lines, cells_z = velocity.shape
    spacing_x = 8.0 * math.pi / (cells_x * lax.axis_size("gx"))
    spacing_z = 3.0 * math.pi / (cells_z * lax.axis_size("gz"))
    dt_step = 0.3 / (1.0 / spacing_x + 1.0 / spacing_z)
    rate_d = decay_rate(alpha_deriv)
    rate_f = decay_rate(alpha_filter)
    size = rows_block
    n_blocks = cells_x // size
    rows = size * lines
    span = cells_x * lines

    kd = kernel_values([1, 2], deriv_taps(spacing_x), alpha_deriv)
    kf = kernel_values([0, 1, 2, 3], filter_taps(), alpha_filter)
    consts = {
        "rate_d": rate_d,
        "ratio_d": float(kd[0] / kd[1]),
        "x_factor": float(-dt_step * kd[1]),
        "rate_f": rate_f,
        "power_f": float(rate_f ** size),
        "k0": float(kf[0]),
        "k1": float(kf[1]),
        "k2": float(kf[2]),
        "k3": float(kf[3]),
    }

    plane = (comps, lines, cells_z)
    big = lambda idx: pl.BlockSpec((comps, size, lines, cells_z), lambda t: (0, idx(t), 0, 0))
    edge = (2,) + plane
    xr_send, xl_send = pl.pallas_call(
        functools.partial(x_edge_body, rate_d),
        grid=(1,),
        in_specs=[
            pl.BlockSpec((comps, near_deriv, lines, cells_z), lambda t: (0, 0, 0, 0)),
            pl.BlockSpec(
                (comps, near_deriv, lines, cells_z), lambda t: (0, cells_x // near_deriv - 1, 0, 0)
            ),
        ],
        out_specs=[whole(edge)] * 2,
        out_shape=[jax.ShapeDtypeStruct(edge, f32)] * 2,
        name="x_edge",
    )(velocity, velocity)
    xl, xr = swap(xr_send, xl_send, "gx")

    group_d = 8
    taps_z = deriv_taps(spacing_z)
    wd = edge_functionals(cells_z, taps_z, alpha_deriv, -dt_step, 2, group_d)
    wd = jnp.asarray(np.concatenate(np_parts(wd), axis=0))
    zr_send, zl_send = pl.pallas_call(
        z_edge_body,
        grid=(n_blocks,),
        in_specs=[big(lambda t: t), whole(wd.shape)],
        out_specs=[pl.BlockSpec((group_d, rows), lambda t: (0, t))] * 2,
        out_shape=[jax.ShapeDtypeStruct((group_d, span), f32)] * 2,
        name="z_edge",
    )(velocity, wd)
    zl, zr = swap(zr_send, zl_send, "gz")

    group_f = 16
    dz = jnp.asarray(band_matrix(cells_z, taps_z, alpha_deriv, -dt_step))
    pd = jnp.asarray(padded_profiles(edge_profiles(cells_z, alpha_deriv, 2, group_d)))
    fz = jnp.asarray(band_matrix(cells_z, filter_taps(), alpha_filter, 1.0))
    wf = edge_functionals(cells_z, filter_taps(), alpha_filter, 1.0, 3, group_f)
    wf = jnp.asarray(np.concatenate(np_parts(wf), axis=0))
    profiles_f = edge_profiles(cells_z, alpha_filter, 3, group_f)
    pf = jnp.asarray(padded_profiles(profiles_f))
    later = lambda t: jnp.maximum(t - n_blocks, 0)
    turn = lambda t: jnp.where(t < n_blocks, n_blocks - 1 - t, t - n_blocks)
    edge3 = (3,) + plane
    advance, q, zr_send, zl_send, xr_part, xl_part = pl.pallas_call(
        functools.partial(advance_body, n_blocks, consts),
        grid=(2 * n_blocks,),
        in_specs=[
            big(turn), big(later), whole(edge), whole(edge),
            pl.BlockSpec((group_d, rows), lambda t: (0, later(t))),
            pl.BlockSpec((group_d, rows), lambda t: (0, later(t))),
            whole(dz.shape), whole(pd.shape), whole(fz.shape), whole(wf.shape),
        ],
        out_specs=[
            big(later), big(later),
            pl.BlockSpec((group_f, rows), lambda t: (0, later(t))),
            pl.BlockSpec((group_f, rows), lambda t: (0, later(t))),
            whole(edge3), whole(edge3),
        ],
        out_shape=[
            jax.ShapeDtypeStruct(velocity.shape, f32),
            jax.ShapeDtypeStruct(velocity.shape, f32),
            jax.ShapeDtypeStruct((group_f, span), f32),
            jax.ShapeDtypeStruct((group_f, span), f32),
            jax.ShapeDtypeStruct(edge3, f32),
            jax.ShapeDtypeStruct(edge3, f32),
        ],
        scratch_shapes=[
            pltpu.VMEM((cells_x,) + plane, f32),
            pltpu.VMEM((2,) + plane, f32),
            pltpu.VMEM((2,) + plane, f32),
            pltpu.VMEM((comps, size, lines, cells_z), f32),
            pltpu.VMEM((3,) + plane, f32),
            pltpu.VMEM(plane, f32),
            pltpu.SMEM((1,), f32),
        ],
        name="advance",
    )(velocity, prior, xl, xr, zl, zr, dz, pd, fz, wf)
    zl, zr = swap(zr_send, zl_send, "gz")

    near = near_filter * lines
    cell = np.arange(cells_x)[:, None, None, None]
    line = (np.arange(lines)[None, :, None, None] == np.arange(lines)[None, None, None, :]) * 1.0
    back_off = cells_x - 3 - cell
    grow = np.where(back_off >= 0, np.power(rate_f, np.maximum(back_off, 0)), 0.0)
    pick = np.concatenate([grow, cell == cells_x - 1, cell == cells_x - 2], axis=2) * 1.0
    right_table = (pick * line).reshape(span, 3 * lines)
    left_table = (pick[::-1] * line).reshape(span, 3 * lines)
    widen = lambda t: np.concatenate([t, np.zeros((near, 128 - t.shape[1]))], axis=1)
    tr = jnp.asarray(widen(right_table[span - near:]), f32)
    tl = jnp.asarray(widen(left_table[:near]), f32)
    pc = jnp.asarray(profiles_f, f32)
    xr_send, xl_send = pl.pallas_call(
        corner_body,
        grid=(1,),
        in_specs=[
            whole(edge3), whole(edge3), whole((group_f, span)), whole((group_f, span)),
            whole(tr.shape), whole(tl.shape), whole(pc.shape),
        ],
        out_specs=[whole(edge3)] * 2,
        out_shape=[jax.ShapeDtypeStruct(edge3, f32)] * 2,
        name="corner",
    )(xr_part, xl_part, zl, zr, tr, tl, pc)
    xl, xr = swap(xr_send, xl_send, "gx")

    early = lambda t: jnp.maximum(n_blocks - 1 - t, 0)
    filtered = pl.pallas_call(
        functools.partial(filter_body, n_blocks, consts),
        grid=(2 * n_blocks,),
        in_specs=[
            big(early), whole(edge3), whole(edge3),
            pl.BlockSpec((group_f, rows), lambda t: (0, early(t))),
            pl.BlockSpec((group_f, rows), lambda t: (0, early(t))),
            whole(pf.shape),
        ],
        out_specs=big(later),
        out_shape=jax.ShapeDtypeStruct(velocity.shape, f32),
        scratch_shapes=[
            pltpu.VMEM((cells_x + 2,) + plane, f32),
            pltpu.VMEM((cells_x,) + plane, f32),
            pltpu.VMEM((3,) + plane, f32),
            pltpu.VMEM((3,) + plane, f32),
        ],
        name="filter",
    )(q, xl, xr, zl, zr, pf)
    return (filtered, advance)


def solution(mesh):
    placed = P(None, "gx", None, "gz")
    return jax.shard_map(
        shards,
        mesh=mesh,
        in_specs=(placed, placed),
        out_specs=(placed, placed),
        check_vma=False,
    )
```

time: 391 us -> 79.8 us (0.20)
  the two profiles are of different devices: /device:TPU:0 before, /device:TPU:7 now
where the time goes in v1:
time: 79.8 us; the launch traced here: 79 us
  Pallas kernels  45.8 us (57%)
  starting transfers between devices  17.7 us (22%)
  waiting for transfers between devices  12.6 us (16%)
  local copies, waits for them, and re-layouts  2.15 us (3%)
    pallas_call x1, Pallas kernels, shards(): pl.pallas_call(functools.partial(advance_body, n_blocks, consts), grid=(2...  21.1 us
    pallas_call x1, Pallas kernels, shards(): pl.pallas_call(functools.partial(filter_body, n_blocks, consts), grid=(2...  12.1 us
    ppermute x4, starting transfers between devices, swap(): lax.ppermute(right, axis, ring(count, 1))  12 us
    pallas_call x1, Pallas kernels, shards(): pl.pallas_call(z_edge_body, grid=(n_blocks,), in_specs=[big(lambda t: t),...  7.28 us
    ppermute x4, waiting for transfers between devices, swap(): lax.ppermute(left, axis, ring(count, -1))  6.68 us
    ppermute x4, waiting for transfers between devices, swap(): lax.ppermute(right, axis, ring(count, 1))  5.9 us
    ppermute x4, starting transfers between devices, swap(): lax.ppermute(left, axis, ring(count, -1))  5.73 us
    pallas_call x1, Pallas kernels, shards(): pl.pallas_call(corner_body, grid=(1,), in_specs=[whole(edge3), whole(edge...  3.14 us
  transfers between devices with their start and end apart: 8, of which 6 were waited for; matrix products, arithmetic and copies ran while one was open for 0% of the time, Pallas kernels for 3%

profile of v1, /device:TPU:7, one launch (start us, length us, event | category | flops | bytes accessed | tf_op | source)
XLA Modules:
  0.0 79.0 jit_solution(6394793652222853651)
XLA Ops:
  0.6 7.3 %z_edge.1 = (f32[8,2048]{1,0:T(8,128)}, f32[8,2048]{1,0:T(8,128)}) custom-call(f32[3,256,8,256]{3,2,1,0:T(8,128)} %v_ref.3, bf16[32,768]{1,0:T(8,128)(2,1)} %constant.18.clone.functional_ref), custom_call_target="tpu_custom_call" | custom-call | tf_op jit(solution)/shard_map/z_edge/pallas_call | solution.py:428
  7.9 4.1 %collective-permute-start.2 = (f32[8,2048]{1,0:T(8,128)}, f32[8,2048]{1,0:T(8,128)S(1)}, u32[]{:S(2)}, u32[]{:S(2)}) collective-permute-start(f32[8,2048]{1,0:T(8,128)} %get-tuple-element.16), channel_id=1, source_target_pairs={{0,1},{1,2},{2,3},{3,4},{4,5},{5,6},{6,7},{7,8},{8,9},{9,10},{10,1... | collective-permute-start | bytes 196616 | tf_op jit(solution)/shard_map/ppermute | solution.py:375
  12.0 0.0 collective-permute-start.3
  12.0 2.1 %x_edge.1 = (f32[2,3,8,256]{3,2,1,0:T(8,128)}, f32[2,3,8,256]{3,2,1,0:T(8,128)}) custom-call(f32[3,256,8,256]{3,2,1,0:T(8,128)} %v_ref.3, f32[3,256,8,256]{3,2,1,0:T(8,128)} %v_ref.3), custom_call_target="tpu_custom_call" | custom-call | tf_op jit(solution)/shard_map/x_edge/pallas_call | solution.py:409
  14.1 0.7 collective-permute-start
  14.9 2.8 %collective-permute-start.1 = (f32[2,3,8,256]{3,2,1,0:T(8,128)}, f32[2,3,8,256]{3,2,1,0:T(8,128)S(1)}, u32[]{:S(2)}, u32[]{:S(2)}) collective-permute-start(f32[2,3,8,256]{3,2,1,0:T(8,128)} %get-tuple-element.15), channel_id=1, source_target_pairs={{0,112},{16,0},{32,16},{48,32},{64,48},{80,64},{96,80},{112,96},{1... | collective-permute-start | bytes 147464 | tf_op jit(solution)/shard_map/ppermute | solution.py:376
  17.7 1.7 %collective-permute-done.xl_ref = f32[2,3,8,256]{3,2,1,0:T(8,128)S(1)} collective-permute-done((f32[2,3,8,256]{3,2,1,0:T(8,128)}, f32[2,3,8,256]{3,2,1,0:T(8,128)S(1)}, u32[]{:S(2)}, u32[]{:S(2)}) %collective-permute-start) | collective-permute-done | bytes 49184 | tf_op jit(solution)/shard_map/ppermute | solution.py:375
  19.4 0.0 copy-start.6
  19.4 0.3 collective-permute-done.1.xr_ref
  19.7 0.0 collective-permute-done.2.zl_ref
  19.7 0.0 copy-start.4
  19.7 0.4 collective-permute-done.3.zr_ref
  20.1 0.0 copy-done.6
  20.1 0.2 copy-done.7
  20.3 0.0 copy-done.4
  20.4 0.0 copy-start.5
  20.4 0.6 copy-done.5
  21.0 21.1 %advance.1 = (f32[3,256,8,256]{3,2,1,0:T(8,128)}, f32[3,256,8,256]{3,2,1,0:T(8,128)}, f32[16,2048]{1,0:T(8,128)}, f32[16,2048]{1,0:T(8,128)}, f32[3,3,8,256]{3,2,1,0:T(8,128)}, /*index=5*/f32[3,3,8,256]{3,2,1,0:T(8,128)}) custom-call(f32[3,256,8,256]{3,2,1,0:T(8,128)} %v_ref.3, f32[3,256,8,256]{3,2,1,0:T(8,128)} %prior_ref.1, f32[2,3,8,256]{3,2,1,0:T(8,128)} %copy-done.6, ...), custom_call_target="tpu_custom_call" | custom-call | tf_op jit(solution)/shard_map/advance/pallas_call | solution.py:449
  42.1 6.3 %collective-permute-start.4 = (f32[16,2048]{1,0:T(8,128)}, f32[16,2048]{1,0:T(8,128)S(1)}, u32[]{:S(2)}, u32[]{:S(2)}) collective-permute-start(f32[16,2048]{1,0:T(8,128)} %get-tuple-element.21), channel_id=1, source_target_pairs={{0,1},{1,2},{2,3},{3,4},{4,5},{5,6},{6,7},{7,8},{8,9},{9,10},{10,1... | collective-permute-start | bytes 393224 | tf_op jit(solution)/shard_map/ppermute | solution.py:375
  48.4 0.0 collective-permute-start.5
  48.4 2.3 %collective-permute-done.4.zl_ref = f32[16,2048]{1,0:T(8,128)S(1)} collective-permute-done((f32[16,2048]{1,0:T(8,128)}, f32[16,2048]{1,0:T(8,128)S(1)}, u32[]{:S(2)}, u32[]{:S(2)}) %collective-permute-start.4) | collective-permute-done | bytes 131104 | tf_op jit(solution)/shard_map/ppermute | solution.py:375
  50.7 6.0 %collective-permute-done.5.zr_ref = f32[16,2048]{1,0:T(8,128)S(1)} collective-permute-done((f32[16,2048]{1,0:T(8,128)}, f32[16,2048]{1,0:T(8,128)S(1)}, u32[]{:S(2)}, u32[]{:S(2)}) %collective-permute-start.5) | collective-permute-done | bytes 131104 | tf_op jit(solution)/shard_map/ppermute | solution.py:376
  56.7 0.0 copy-done
  56.7 0.6 copy-done.1
  57.3 3.1 %corner.1 = (f32[3,3,8,256]{3,2,1,0:T(8,128)}, f32[3,3,8,256]{3,2,1,0:T(8,128)}) custom-call(f32[3,3,8,256]{3,2,1,0:T(8,128)} %get-tuple-element.19.xright_ref, f32[3,3,8,256]{3,2,1,0:T(8,128)} %get-tuple-element.20.xleft_ref, f32[16,2048]{1,0:T(8,128)} %copy-done, f32[16,2048]{1,0:T(8,128)} %copy-done.1, f32[768,128]{1,0:T(8,128)} %constant.24.clone.tr_ref, ...), custom_call_target="tpu_custom_call" | custom-call | tf_op jit(solution)/shard_map/corner/pallas_call | solution.py:497
  60.4 0.9 %collective-permute-start.6 = (f32[3,3,8,256]{3,2,1,0:T(8,128)}, f32[3,3,8,256]{3,2,1,0:T(8,128)S(1)}, u32[]{:S(2)}, u32[]{:S(2)}) collective-permute-start(f32[3,3,8,256]{3,2,1,0:T(8,128)} %get-tuple-element.23), channel_id=1, source_target_pairs={{0,16},{16,32},{32,48},{48,64},{64,80},{80,96},{96,112},{112,0},{1... | collective-permute-start | bytes 221192 | tf_op jit(solution)/shard_map/ppermute | solution.py:375
  61.3 2.9 %collective-permute-start.7 = (f32[3,3,8,256]{3,2,1,0:T(8,128)}, f32[3,3,8,256]{3,2,1,0:T(8,128)S(1)}, u32[]{:S(2)}, u32[]{:S(2)}) collective-permute-start(f32[3,3,8,256]{3,2,1,0:T(8,128)} %get-tuple-element.24), channel_id=1, source_target_pairs={{0,112},{16,0},{32,16},{48,32},{64,48},{80,64},{96,80},{112,96},{1... | collective-permute-start | bytes 221192 | tf_op jit(solution)/shard_map/ppermute | solution.py:376
  64.2 1.9 %collective-permute-done.6.xl_ref = f32[3,3,8,256]{3,2,1,0:T(8,128)S(1)} collective-permute-done((f32[3,3,8,256]{3,2,1,0:T(8,128)}, f32[3,3,8,256]{3,2,1,0:T(8,128)S(1)}, u32[]{:S(2)}, u32[]{:S(2)}) %collective-permute-start.6) | collective-permute-done | bytes 73760 | tf_op jit(solution)/shard_map/ppermute | solution.py:375
  66.2 0.0 collective-permute-done.7.xr_ref
  66.2 0.6 copy-done.2
  66.8 0.0 copy-done.3
  66.8 12.1 %filter.1 = f32[3,256,8,256]{3,2,1,0:T(8,128)} custom-call(f32[3,256,8,256]{3,2,1,0:T(8,128)} %get-tuple-element.18.q_ref, f32[3,3,8,256]{3,2,1,0:T(8,128)} %copy-done.2, f32[3,3,8,256]{3,2,1,0:T(8,128)} %copy-done.3, f32[16,2048]{1,0:T(8,128)} %copy-done, f32[16,2048]{1,0:T(8,128)} %copy-done.1, bf16[3,128,256]{2,1,0:T(8,128)(2,1)} %constant.23.clone.pz_ref), custom_call_target="tpu_custom_call" | custom-call | tf_op jit(solution)/shard_map/filter/pallas_call | solution.py:511
  (5 shorter events, 0.0 us)
Async XLA Ops:
  7.9 11.8 %collective-permute-start.2 = (f32[8,2048]{1,0:T(8,128)}, f32[8,2048]{1,0:T(8,128)S(1)}, u32[]{:S(2)}, u32[]{:S(2)}) collective-permute-start(f32[8,2048]{1,0:T(8,128)} %get-tuple-element.16), channel_id=1, source_target_pairs={{0,1},{1,2},{2,3},{3,4},{4,5},{5,6},{6,7},{7,8},{8,9},{9,10},{10,1... | collective-permute-start | bytes 196616 | tf_op jit(solution)/shard_map/ppermute | solution.py:375
  12.0 8.1 %collective-permute-start.3 = (f32[8,2048]{1,0:T(8,128)}, f32[8,2048]{1,0:T(8,128)S(1)}, u32[]{:S(2)}, u32[]{:S(2)}) collective-permute-start(f32[8,2048]{1,0:T(8,128)} %get-tuple-element.17), channel_id=1, source_target_pairs={{0,15},{1,0},{2,1},{3,2},{4,3},{5,4},{6,5},{7,6},{8,7},{9,8},{10,9... | collective-permute-start | bytes 196616 | tf_op jit(solution)/shard_map/ppermute | solution.py:376
  14.1 5.3 %collective-permute-start = (f32[2,3,8,256]{3,2,1,0:T(8,128)}, f32[2,3,8,256]{3,2,1,0:T(8,128)S(1)}, u32[]{:S(2)}, u32[]{:S(2)}) collective-permute-start(f32[2,3,8,256]{3,2,1,0:T(8,128)} %get-tuple-element.14), channel_id=1, source_target_pairs={{0,16},{16,32},{32,48},{48,64},{64,80},{80,96},{96,112},{112,0},{1... | collective-permute-start | bytes 147464 | tf_op jit(solution)/shard_map/ppermute | solution.py:375
  14.9 4.8 %collective-permute-start.1 = (f32[2,3,8,256]{3,2,1,0:T(8,128)}, f32[2,3,8,256]{3,2,1,0:T(8,128)S(1)}, u32[]{:S(2)}, u32[]{:S(2)}) collective-permute-start(f32[2,3,8,256]{3,2,1,0:T(8,128)} %get-tuple-element.15), channel_id=1, source_target_pairs={{0,112},{16,0},{32,16},{48,32},{64,48},{80,64},{96,80},{112,96},{1... | collective-permute-start | bytes 147464 | tf_op jit(solution)/shard_map/ppermute | solution.py:376
  19.4 0.7 copy-start.6
  19.7 0.6 copy-start.7
  19.7 0.6 copy-start.4
  20.4 0.6 copy-start.5
  42.1 8.6 %collective-permute-start.4 = (f32[16,2048]{1,0:T(8,128)}, f32[16,2048]{1,0:T(8,128)S(1)}, u32[]{:S(2)}, u32[]{:S(2)}) collective-permute-start(f32[16,2048]{1,0:T(8,128)} %get-tuple-element.21), channel_id=1, source_target_pairs={{0,1},{1,2},{2,3},{3,4},{4,5},{5,6},{6,7},{7,8},{8,9},{9,10},{10,1... | collective-permute-start | bytes 393224 | tf_op jit(solution)/shard_map/ppermute | solution.py:375
  48.4 8.2 %collective-permute-start.5 = (f32[16,2048]{1,0:T(8,128)}, f32[16,2048]{1,0:T(8,128)S(1)}, u32[]{:S(2)}, u32[]{:S(2)}) collective-permute-start(f32[16,2048]{1,0:T(8,128)} %get-tuple-element.22), channel_id=1, source_target_pairs={{0,15},{1,0},{2,1},{3,2},{4,3},{5,4},{6,5},{7,6},{8,7},{9,8},{10,9... | collective-permute-start | bytes 393224 | tf_op jit(solution)/shard_map/ppermute | solution.py:376
  50.7 6.0 %copy-start = (f32[16,2048]{1,0:T(8,128)}, f32[16,2048]{1,0:T(8,128)S(1)}, u32[]{:S(2)}) copy-start(f32[16,2048]{1,0:T(8,128)S(1)} %collective-permute-done.4.zl_ref) | copy-start | bytes 393220
  56.6 0.6 copy-start.1
  60.4 5.7 %collective-permute-start.6 = (f32[3,3,8,256]{3,2,1,0:T(8,128)}, f32[3,3,8,256]{3,2,1,0:T(8,128)S(1)}, u32[]{:S(2)}, u32[]{:S(2)}) collective-permute-start(f32[3,3,8,256]{3,2,1,0:T(8,128)} %get-tuple-element.23), channel_id=1, source_target_pairs={{0,16},{16,32},{32,48},{48,64},{64,80},{80,96},{96,112},{112,0},{1... | collective-permute-start | bytes 221192 | tf_op jit(solution)/shard_map/ppermute | solution.py:375
  61.3 4.8 %collective-permute-start.7 = (f32[3,3,8,256]{3,2,1,0:T(8,128)}, f32[3,3,8,256]{3,2,1,0:T(8,128)S(1)}, u32[]{:S(2)}, u32[]{:S(2)}) collective-permute-start(f32[3,3,8,256]{3,2,1,0:T(8,128)} %get-tuple-element.24), channel_id=1, source_target_pairs={{0,112},{16,0},{32,16},{48,32},{64,48},{80,64},{96,80},{112,96},{1... | collective-permute-start | bytes 221192 | tf_op jit(solution)/shard_map/ppermute | solution.py:376
  66.2 0.6 copy-start.2
  66.2 0.7 copy-start.3
